TPU v7x, 128 devices: a whole 4x4x4 slice. The times are simulated.
128 devices in a mesh: variant: 8 (over z_lo, x), vocab: 16 (over y, z_hi, core).
Axes of the slice: x: 4, y: 4, z: 4 (z_hi: 2, z_lo: 2; z = z_hi * 2 + z_lo), core: 2. Of those that a mesh axis runs over, the one named last changes fastest.
Arguments:
- teacher_hidden: bfloat16 [8, 256, 4096], P(None, None, ('variant', 'vocab')), may hold values from -24 to 24
- teacher_weight: bfloat16 [4096, 64128], P(None, ('vocab', 'variant')), may hold values from -1 to 1
- variant_ids: int32 [8], replicated, may hold values from 0 to 13
- temps: float32 [14], replicated, may hold values from 0.7 to 1.5
- student_hidden: bfloat16 [256, 2048], P(None, 'variant'), may hold values from -24 to 24
- student_weight: bfloat16 [2048, 64128], P('variant', 'vocab'), may hold values from -1 to 1
- token_ids: int32 [256], P('variant'), may hold values from 0 to 64127
- loss_mask: int32 [256], P('variant'), may hold values 0 or 1
Outputs:
- token_loss: float32 [256], P('variant')
- student_grad: float32 [2048, 64128], P('variant', 'vocab')
All inputs are finite; a program needn't handle non-finite values. No bound on the sum of `loss_mask` on one device may be relied on, other than what follows from the above.
Results may differ from a plain program's by a relative error of at most 0.0025.
Values may be sent and summed in bfloat16 or wider, within the bound.
No kernel may reach another device: no remote copies, remote signals or barrier semaphores. Data moves between devices by JAX's collectives and lax.ppermute only.
A program may use at most 192 MiB of HBM per device.

v0:
```python
import jax
import jax.numpy as jnp
from jax import lax
from jax.sharding import PartitionSpec as P

mix_weight = 0.5
loss_scale = 4096.0


def on_device(
    teacher_hidden,
    teacher_weight,
    variant_ids,
    temps,
    student_hidden,
    student_weight,
    token_ids,
    loss_mask,
):
    n_variant = lax.axis_size("variant")
    categories = jnp.arange(temps.shape[0], dtype=jnp.int32)
    taus = jnp.sum(
        jnp.where(variant_ids[:, None] == categories[None, :], temps[None, :], 0.0), axis=1
    )
    hidden_all = lax.all_gather(teacher_hidden, ("variant", "vocab"), axis=2, tiled=True)
    scaled = (
        jnp.einsum("vtd,dc->vtc", hidden_all, teacher_weight, preferred_element_type=jnp.float32)
        / taus[:, None, None]
    )
    local_max = jnp.max(scaled, axis=2)
    top = lax.pmax(local_max, ("variant", "vocab"))
    total = lax.psum(jnp.sum(jnp.exp(scaled - top[:, :, None]), axis=2), ("variant", "vocab"))
    probs = jnp.exp(scaled - top[:, :, None]) / total[:, :, None]
    averaged_cols = jnp.sum(probs, axis=0) / n_variant
    averaged = lax.all_to_all(
        averaged_cols.astype(jnp.bfloat16), "variant", split_axis=0, concat_axis=1, tiled=True
    ).astype(averaged_cols.dtype)
    block = student_hidden
    logits = lax.psum_scatter(
        jnp.dot(block, student_weight, preferred_element_type=jnp.float32),
        "variant",
        scatter_dimension=0,
        tiled=True,
    )
    local_max = jnp.max(logits, axis=1)
    top = lax.pmax(local_max, "vocab")
    total = lax.psum(jnp.sum(jnp.exp(logits - top[:, None]), axis=1), "vocab")
    log_probs = logits - (top + jnp.log(total))[:, None]
    probs_student = jnp.exp(log_probs)
    columns = lax.axis_index("vocab") * logits.shape[1] + jnp.arange(
        logits.shape[1], dtype=jnp.int32
    )
    onehot = token_ids[:, None] == columns[None, :]
    soft, hard = lax.psum(
        (jnp.sum(averaged * log_probs, axis=1), jnp.sum(jnp.where(onehot, log_probs, 0.0), axis=1)),
        "vocab",
    )
    maskf = loss_mask.astype(jnp.float32)
    token_loss = maskf * (-mix_weight * soft - (1.0 - mix_weight) * hard)
    error = (
        loss_scale
        * maskf[:, None]
        * (probs_student - mix_weight * averaged - (1.0 - mix_weight) * onehot.astype(jnp.float32))
    ).astype(jnp.bfloat16)
    block = student_hidden
    student_grad = lax.dot_general(
        block,
        lax.all_gather(error, "variant", axis=0, tiled=True),
        (((0,), (0,)), ((), ())),
        preferred_element_type=jnp.float32,
    )
    return (token_loss, student_grad)


def solution(mesh):
    in_specs = (
        P(None, None, ("variant", "vocab")),
        P(None, ("vocab", "variant")),
        P(),
        P(),
        P(None, "variant"),
        P("variant", "vocab"),
        P("variant"),
        P("variant"),
    )
    out_specs = (P("variant"), P("variant", "vocab"))
    return jax.shard_map(
        on_device, mesh=mesh, in_specs=in_specs, out_specs=out_specs, check_vma=False
    )
```

profile of v0, /device:TPU:0, one launch (start us, length us, event | category | flops | bytes accessed | tf_op | source)
XLA Modules:
  0.0 505.8 jit_solution(16824957268856968234)
XLA Ops:
  8.0 0.0 copy-start
  8.0 0.0 reduce-scatter.2.cloned.1.call-start
  8.1 1.5 copy-done
  9.6 3.6 fusion.11
  13.2 0.0 reduce-scatter.2.cloned.1.call-update
  13.2 0.0 all-gather.3.cloned.1.call-start
  13.2 0.5 all-gather.3.cloned.1.call-update
  13.8 0.2 select_reduce_fusion
  14.0 60.6 %reduce-scatter.2.cloned.1.call-done = f32[32,4008]{1,0:T(8,128)} async-done(((f32[256,4008]{1,0:T(8,128)}), f32[32,4008]{1,0:T(8,128)}) %reduce-scatter.2.cloned.1.call-update) | async-done | bytes 513040 | tf_op jit(solution)/shard_map/reduce_scatter | solution.py:39
  74.6 1.2 reduce_max.19
  75.8 38.9 %pmax.15 = f32[32]{0:T(128)S(1)} all-reduce(f32[32]{0:T(128)S(1)} %reduce_max.19), channel_id=1, replica_groups=mesh['variant'=8,'vocab'=16] {'vocab'}, use_global_device_ids=true, to_apply=%region_8.9 | all-reduce | flops 32 | bytes 256 | tf_op jit(solution)/shard_map/pmax | solution.py:46
  114.7 151.1 %all-gather.3.cloned.1.call-done = bf16[8,256,4096]{1,2,0:T(8,128)(2,1)} async-done(((bf16[8,256,32]{1,2,0:T(8,128)(2,1)}), bf16[8,256,4096]{1,2,0:T(8,128)(2,1)}) %all-gather.3.cloned.1.call-update) | async-done | bytes 16777232 | tf_op jit(solution)/shard_map/all_gather | solution.py:25
  265.9 14.8 %fusion.10 = (f32[8,256]{1,0:T(8,128)S(1)}, f32[8,256,501]{1,2,0:T(8,128)}) fusion(f32[8]{0:T(128)S(1)} %select_reduce_fusion, bf16[8,256,4096]{1,2,0:T(8,128)(2,1)} %all-gather.3.cloned.1.call-done, bf16[4096,501]{0,1:T(8,128)(2,1)} %param.9), kind=kOutput, calls=%fused_computation.23 | convolution fusion | flops 8407435264 | bytes 24993824 | tf_op jit(solution)/shard_map/vtd,dc->vtc/dot_general | solution.py:27
  280.6 62.0 %pmax.14 = f32[8,256]{1,0:T(8,128)S(1)} all-reduce(f32[8,256]{1,0:T(8,128)S(1)} %get-tuple-element.7), channel_id=1, replica_groups=mesh['variant'=8,'vocab'=16] {'variant','vocab'}, use_global_device_ids=true, to_apply=%region_2.3 | all-reduce | flops 2048 | bytes 16384 | tf_op jit(solution)/shard_map/pmax | solution.py:31
  342.6 2.7 fusion.2
  345.4 64.6 %psum.28 = f32[8,256]{1,0:T(8,128)S(1)} all-reduce(f32[8,256]{1,0:T(8,128)S(1)} %fusion.2), channel_id=1, replica_groups=mesh['variant'=8,'vocab'=16] {'variant','vocab'}, use_global_device_ids=true, to_apply=%region_4.5 | all-reduce | flops 2048 | bytes 16384 | tf_op jit(solution)/shard_map/psum | solution.py:32
  410.0 2.9 divide_reduce_fusion
  412.9 0.0 copy-start.2
  413.0 0.8 copy.13
  413.8 3.4 all-to-all-start
  417.3 0.0 all-gather.5.cloned.1.call-start
  417.3 0.3 exponential_reduce_fusion
  417.6 34.1 %psum.29 = f32[32]{0:T(128)S(1)} all-reduce(f32[32]{0:T(128)S(1)} %exponential_reduce_fusion), channel_id=1, replica_groups=mesh['variant'=8,'vocab'=16] {'vocab'}, use_global_device_ids=true, to_apply=%region_10.11 | all-reduce | flops 32 | bytes 256 | tf_op jit(solution)/shard_map/psum | solution.py:47
  451.7 0.1 convert_bitcast_fusion
  451.8 1.1 copy.14
  452.9 1.4 reshape.27
  454.2 1.1 multiply_reduce_fusion
  455.4 0.0 all-gather.5.cloned.1.call-update
  455.4 33.7 %all-reduce = (f32[32]{0:T(128)S(1)}, f32[32]{0:T(128)S(1)}) all-reduce(f32[32]{0:T(128)S(1)} %get-tuple-element.3, f32[32]{0:T(128)S(1)} %get-tuple-element.2), channel_id=1, replica_groups=mesh['variant'=8,'vocab'=16] {'vocab'}, use_global_device_ids=true, to_apply=%region_14.15 | all-reduce | flops 64 | bytes 512 | tf_op jit(solution)/shard_map/psum | solution.py:54
  489.1 0.5 subtract_multiply_fusion
  489.6 4.4 all-gather.5.cloned.1.call-done
  494.0 4.3 convolution_bitcast_fusion
  (16 shorter events, 0.1 us)
Async XLA Ops:
  8.0 1.6 copy-start
  8.0 5.8 %copy-start.5 = (f32[14]{0:T(128)S(1)}, f32[14]{0:T(128)}, u32[]{:S(2)}) copy-start(f32[14]{0:T(128)} %param.11) | copy-start | bytes 172
  8.0 5.8 %copy-start.6 = (s32[8]{0:T(128)S(1)}, s32[8]{0:T(128)}, u32[]{:S(2)}) copy-start(s32[8]{0:T(128)} %param.10) | copy-start | bytes 100
  8.0 5.9 %copy-start.4 = (s32[32]{0:T(128)S(1)}, s32[32]{0:T(128)}, u32[]{:S(2)}) copy-start(s32[32]{0:T(128)} %param.15) | copy-start | bytes 388
  8.0 66.6 %reduce-scatter.2.cloned.1.call-start = ((), (), s32[]{:S(2)}) async-start(), calls=%async_computation.3 | async-start | bytes 4718592 | tf_op jit(solution)/shard_map/reduce_scatter | solution.py:39
  13.2 252.7 %all-gather.3.cloned.1.call-start = ((), (), s32[]{:S(2)}) async-start(), calls=%async_computation.2 | async-start | bytes 16908288 | tf_op jit(solution)/shard_map/all_gather | solution.py:25
  345.4 71.9 %copy-start.1 = (f32[32,4008]{1,0:T(8,128)S(1)}, f32[32,4008]{1,0:T(8,128)}, u32[]{:S(2)}) copy-start(f32[32,4008]{1,0:T(8,128)} %reduce-scatter.2.cloned.1.call-done) | copy-start | bytes 1539076
  410.0 44.2 %copy-start.3 = (s32[32]{0:T(128)S(1)}, s32[32]{0:T(128)}, u32[]{:S(2)}) copy-start(s32[32]{0:T(128)} %param.14) | copy-start | bytes 388
  412.9 81.1 %copy-start.2 = (bf16[256,256]{1,0:T(8,128)(2,1)S(1)}, bf16[256,256]{1,0:T(8,128)(2,1)}, u32[]{:S(2)}) copy-start(bf16[256,256]{1,0:T(8,128)(2,1)} %param.12) | copy-start | bytes 393220
  413.8 37.9 %all-to-all-start = ((bf16[8,32,501]{2,1,0:T(8,128)(2,1)}), bf16[8,32,501]{2,1,0:T(8,128)(2,1)S(1)}, u32[]{:S(2)}, u32[]{:S(2)}) async-start(bf16[8,32,501]{2,1,0:T(8,128)(2,1)} %bitcast.1), calls=%async_computation | async-start | bytes 524288 | tf_op jit(solution)/shard_map/all_to_all | solution.py:35
  417.3 76.8 %all-gather.5.cloned.1.call-start = ((), (), s32[]{:S(2)}) async-start(), calls=%async_computation.4 | async-start | bytes 2359296 | tf_op jit(solution)/shard_map/all_gather | solution.py:68
Sparse Core Ops, SparseCore 0:
  13.3 61.2 reduce-scatter.1
  455.5 38.4 all-gather.4
Sparse Core Ops, SparseCore 1:
  15.4 250.4 all-gather.2
where the time goes:
time: 506 us
  blocking collectives  233 us (46%)
  waiting for transfers between devices  217 us (43%)
  matrix products  22.7 us (4%)
  between operations  15.6 us (3%)
  other arithmetic  9.06 us (2%)
    all_gather x1, waiting for transfers between devices, on_device(): lax.all_gather(teacher_hidden, ('variant', 'vocab'), axis=2, tiled=True)  151 us
    psum x1, blocking collectives, on_device(): lax.psum(jnp.sum(jnp.exp(scaled - top[:, :, None]), axis=2), ('variant',...  64.6 us
    pmax x1, blocking collectives, on_device(): top = lax.pmax(local_max, ('variant', 'vocab'))  62 us
    reduce_scatter x1, waiting for transfers between devices, on_device(): lax.psum_scatter(jnp.dot(block, student_weight, preferred_element_type=jn...  60.6 us
    pmax x1, blocking collectives, on_device(): top = lax.pmax(local_max, 'vocab')  38.9 us
    psum x1, blocking collectives, on_device(): total = lax.psum(jnp.sum(jnp.exp(logits - top[:, None]), axis=1), 'vocab')  34.1 us
    psum x1, blocking collectives, on_device(): lax.psum((jnp.sum(averaged * log_probs, axis=1), jnp.sum(jnp.where(onehot...  33.7 us
    dot_general x1, matrix products, on_device(): jnp.einsum('vtd,dc->vtc', hidden_all, teacher_weight, preferred_element_t...  14.8 us
  transfers between devices with their start and end apart: 4, of which 3 were waited for; matrix products, arithmetic and copies ran while one was open for 0% of the time, Pallas kernels for 0%

commit v1 on v0

--- a/solution.py
+++ b/solution.py
@@ -2,6 +2,7 @@
 import jax.numpy as jnp
 from jax import lax
 from jax.sharding import PartitionSpec as P
+from jax.lax import psum
 
 mix_weight = 0.5
 loss_scale = 4096.0
@@ -29,7 +30,10 @@
     )
     local_max = jnp.max(scaled, axis=2)
     top = lax.pmax(local_max, ("variant", "vocab"))
-    total = lax.psum(jnp.sum(jnp.exp(scaled - top[:, :, None]), axis=2), ("variant", "vocab"))
+    total = psum(
+        psum(jnp.sum(jnp.exp(scaled - top[:, :, None]), axis=2), axis_name="variant"),
+        axis_name="vocab",
+    )
     probs = jnp.exp(scaled - top[:, :, None]) / total[:, :, None]
     averaged_cols = jnp.sum(probs, axis=0) / n_variant
     averaged = lax.all_to_all(

time: 506 us -> 465 us (0.919)
  blocking collectives: 233 us -> 187 us
    psum x2, blocking collectives: 98.7 us -> 52.3 us  [the longest x1 34.1 us: on_device(): psum(psum(jnp.sum(jnp.exp(scaled - top[:, :, None]), axis=2), axis_name='...]
    all_to_all x1, waiting for transfers between devices: 0.01 us -> 7.36 us  [on_device(): lax.all_to_all(averaged_cols.astype(jnp.bfloat16), 'variant', split_axis=...]
  transfers between devices with their start and end apart: 4 -> 4, of which waited for: 3 -> 4; matrix products, arithmetic and copies ran while one was open for 0% -> 1% of each run, Pallas kernels for 0% -> 0%
where the time goes in v1:
time: 465 us
  waiting for transfers between devices  221 us (48%)
  blocking collectives  187 us (40%)
  matrix products  22.7 us (5%)
  between operations  15.7 us (3%)
  other arithmetic  10.1 us (2%)
  local copies, waits for them, and re-layouts  4.83 us (1%)
    all_gather x1, waiting for transfers between devices, on_device(): lax.all_gather(teacher_hidden, ('variant', 'vocab'), axis=2, tiled=True)  150 us
    pmax x1, blocking collectives, on_device(): top = lax.pmax(local_max, ('variant', 'vocab'))  62.3 us
    reduce_scatter x1, waiting for transfers between devices, on_device(): lax.psum_scatter(jnp.dot(block, student_weight, preferred_element_type=jn...  60.6 us
    pmax x1, blocking collectives, on_device(): top = lax.pmax(local_max, 'vocab')  38.9 us
    psum x1, blocking collectives, on_device(): psum(psum(jnp.sum(jnp.exp(scaled - top[:, :, None]), axis=2), axis_name='...  34.1 us
    psum x1, blocking collectives, on_device(): lax.psum((jnp.sum(averaged * log_probs, axis=1), jnp.sum(jnp.where(onehot...  33.5 us
    psum x1, blocking collectives, on_device(): psum(jnp.sum(jnp.exp(scaled - top[:, :, None]), axis=2), axis_name='varia...  18.2 us
    dot_general x1, matrix products, on_device(): jnp.einsum('vtd,dc->vtc', hidden_all, teacher_weight, preferred_element_t...  14.8 us
  transfers between devices with their start and end apart: 4, of which 4 were waited for; matrix products, arithmetic and copies ran while one was open for 1% of the time, Pallas kernels for 0%

profile of v1, /device:TPU:0, one launch (start us, length us, event | category | flops | bytes accessed | tf_op | source)
XLA Modules:
  0.0 464.5 jit_solution(9619066202160707379)
XLA Ops:
  8.0 0.0 copy-start
  8.0 0.0 reduce-scatter.2.cloned.1.call-start
  8.1 1.5 copy-done
  9.6 3.6 fusion.11
  13.2 0.0 reduce-scatter.2.cloned.1.call-update
  13.2 0.0 all-gather.3.cloned.1.call-start
  13.2 0.5 all-gather.3.cloned.1.call-update
  13.8 0.2 select_reduce_fusion
  14.0 60.6 %reduce-scatter.2.cloned.1.call-done = f32[32,4008]{1,0:T(8,128)} async-done(((f32[256,4008]{1,0:T(8,128)}), f32[32,4008]{1,0:T(8,128)}) %reduce-scatter.2.cloned.1.call-update) | async-done | bytes 513040 | tf_op jit(solution)/shard_map/reduce_scatter | solution.py:43
  74.6 1.2 reduce_max.19
  75.8 38.9 %pmax.15 = f32[32]{0:T(128)S(1)} all-reduce(f32[32]{0:T(128)S(1)} %reduce_max.19), channel_id=1, replica_groups=mesh['variant'=8,'vocab'=16] {'vocab'}, use_global_device_ids=true, to_apply=%region_9.10 | all-reduce | flops 32 | bytes 256 | tf_op jit(solution)/shard_map/pmax | solution.py:50
  114.7 1.3 exponential_reduce_fusion
  116.0 149.5 %all-gather.3.cloned.1.call-done = bf16[8,256,4096]{1,2,0:T(8,128)(2,1)} async-done(((bf16[8,256,32]{1,2,0:T(8,128)(2,1)}), bf16[8,256,4096]{1,2,0:T(8,128)(2,1)}) %all-gather.3.cloned.1.call-update) | async-done | bytes 16777232 | tf_op jit(solution)/shard_map/all_gather | solution.py:26
  265.5 14.8 %fusion.10 = (f32[8,256]{1,0:T(8,128)S(1)}, f32[8,256,501]{1,2,0:T(8,128)}) fusion(f32[8]{0:T(128)S(1)} %select_reduce_fusion, bf16[8,256,4096]{1,2,0:T(8,128)(2,1)} %all-gather.3.cloned.1.call-done, bf16[4096,501]{0,1:T(8,128)(2,1)} %param.9), kind=kOutput, calls=%fused_computation.23 | convolution fusion | flops 8407435264 | bytes 24993824 | tf_op jit(solution)/shard_map/vtd,dc->vtc/dot_general | solution.py:28
  280.3 62.3 %pmax.14 = f32[8,256]{1,0:T(8,128)S(1)} all-reduce(f32[8,256]{1,0:T(8,128)S(1)} %get-tuple-element.9), channel_id=1, replica_groups=mesh['variant'=8,'vocab'=16] {'variant','vocab'}, use_global_device_ids=true, to_apply=%region_2.3 | all-reduce | flops 2048 | bytes 16384 | tf_op jit(solution)/shard_map/pmax | solution.py:32
  342.6 2.7 fusion.2
  345.3 18.2 %psum.35 = f32[8,256]{1,0:T(8,128)S(1)} all-reduce(f32[8,256]{1,0:T(8,128)S(1)} %fusion.2), channel_id=1, replica_groups=mesh['variant'=8,'vocab'=16] {'variant'}, use_global_device_ids=true, to_apply=%region_4.5 | all-reduce | flops 2048 | bytes 16384 | tf_op jit(solution)/shard_map/psum | solution.py:34
  363.5 34.1 %all-reduce.1 = (f32[8,256]{1,0:T(8,128)S(1)}, f32[32]{0:T(128)S(1)}) all-reduce(f32[8,256]{1,0:T(8,128)S(1)} %psum.35, f32[32]{0:T(128)S(1)} %exponential_reduce_fusion), channel_id=1, replica_groups=mesh['variant'=8,'vocab'=16] {'vocab'}, use_global_device_ids=true, to_apply=%region_5.6 | all-reduce | flops 2080 | bytes 16640 | tf_op jit(solution)/shard_map/psum | solution.py:33
  397.7 0.0 copy-start.3
  397.7 3.0 divide_reduce_fusion
  400.7 0.8 copy.13
  401.6 3.4 all-to-all-start
  405.0 0.0 all-gather.5.cloned.1.call-start
  405.1 7.4 %all-to-all-done = bf16[8,32,501]{2,1,0:T(8,128)(2,1)S(1)} async-done(((bf16[8,32,501]{2,1,0:T(8,128)(2,1)}), bf16[8,32,501]{2,1,0:T(8,128)(2,1)S(1)}, u32[]{:S(2)}, u32[]{:S(2)}) %all-to-all-start) | async-done | bytes 256544 | tf_op jit(solution)/shard_map/all_to_all | solution.py:39
  412.5 1.1 copy.14
  413.6 1.4 reshape.27
  415.0 1.1 multiply_reduce_fusion
  416.1 0.0 all-gather.5.cloned.1.call-update
  416.1 33.5 %all-reduce = (f32[32]{0:T(128)S(1)}, f32[32]{0:T(128)S(1)}) all-reduce(f32[32]{0:T(128)S(1)} %get-tuple-element.3, f32[32]{0:T(128)S(1)} %get-tuple-element.2), channel_id=1, replica_groups=mesh['variant'=8,'vocab'=16] {'vocab'}, use_global_device_ids=true, to_apply=%region_15.16 | all-reduce | flops 64 | bytes 512 | tf_op jit(solution)/shard_map/psum | solution.py:58
  449.6 0.5 subtract_multiply_fusion
  450.1 2.6 all-gather.5.cloned.1.call-done
  452.8 4.3 convolution_bitcast_fusion
  (16 shorter events, 0.1 us)
Async XLA Ops:
  8.0 1.6 copy-start
  8.0 5.7 %copy-start.5 = (f32[14]{0:T(128)S(1)}, f32[14]{0:T(128)}, u32[]{:S(2)}) copy-start(f32[14]{0:T(128)} %param.11) | copy-start | bytes 172
  8.0 5.7 %copy-start.6 = (s32[8]{0:T(128)S(1)}, s32[8]{0:T(128)}, u32[]{:S(2)}) copy-start(s32[8]{0:T(128)} %param.10) | copy-start | bytes 100
  8.0 5.9 %copy-start.4 = (s32[32]{0:T(128)S(1)}, s32[32]{0:T(128)}, u32[]{:S(2)}) copy-start(s32[32]{0:T(128)} %param.15) | copy-start | bytes 388
  8.0 66.6 %reduce-scatter.2.cloned.1.call-start = ((), (), s32[]{:S(2)}) async-start(), calls=%async_computation.3 | async-start | bytes 4718592 | tf_op jit(solution)/shard_map/reduce_scatter | solution.py:43
  13.2 252.4 %all-gather.3.cloned.1.call-start = ((), (), s32[]{:S(2)}) async-start(), calls=%async_computation.2 | async-start | bytes 16908288 | tf_op jit(solution)/shard_map/all_gather | solution.py:26
  397.6 17.3 %copy-start.1 = (f32[32,4008]{1,0:T(8,128)S(1)}, f32[32,4008]{1,0:T(8,128)}, u32[]{:S(2)}) copy-start(f32[32,4008]{1,0:T(8,128)} %reduce-scatter.2.cloned.1.call-done) | copy-start | bytes 1539076
  397.7 17.3 %copy-start.3 = (s32[32]{0:T(128)S(1)}, s32[32]{0:T(128)}, u32[]{:S(2)}) copy-start(s32[32]{0:T(128)} %param.14) | copy-start | bytes 388
  400.6 52.1 %copy-start.2 = (bf16[256,256]{1,0:T(8,128)(2,1)S(1)}, bf16[256,256]{1,0:T(8,128)(2,1)}, u32[]{:S(2)}) copy-start(bf16[256,256]{1,0:T(8,128)(2,1)} %param.12) | copy-start | bytes 393220
  401.6 10.9 %all-to-all-start = ((bf16[8,32,501]{2,1,0:T(8,128)(2,1)}), bf16[8,32,501]{2,1,0:T(8,128)(2,1)S(1)}, u32[]{:S(2)}, u32[]{:S(2)}) async-start(bf16[8,32,501]{2,1,0:T(8,128)(2,1)} %bitcast.1), calls=%async_computation | async-start | bytes 524288 | tf_op jit(solution)/shard_map/all_to_all | solution.py:39
  405.0 47.8 %all-gather.5.cloned.1.call-start = ((), (), s32[]{:S(2)}) async-start(), calls=%async_computation.4 | async-start | bytes 2359296 | tf_op jit(solution)/shard_map/all_gather | solution.py:72
Sparse Core Ops, SparseCore 0:
  13.3 61.2 reduce-scatter.1
  416.2 36.4 all-gather.4
Sparse Core Ops, SparseCore 1:
  15.4 250.1 all-gather.2
